TPU v7x, 32 devices: a whole 2x2x4 slice. The times are simulated.
32 devices in a mesh: dp: 1, center: 32 (over z, y, x, core).
Axes of the slice: x: 2, y: 2, z: 4, core: 2. Of those that a mesh axis runs over, the one named last changes fastest.
Arguments:
- embeddings: bfloat16 [1024, 2048], P('dp', 'center'), may hold values from -6 to 6
- first_weight: bfloat16 [2048, 2048], P(None, 'center'), may hold values from -0.125 to 0.125
- first_bias: float32 [2048], P('center'), may hold values from -3 to 3
- second_weight: bfloat16 [2048, 512], P('center'), may hold values from -0.1875 to 0.1875
- centers: bfloat16 [65536, 512], P('center'), may hold values from -4 to 4
- coefficients: bfloat16 [65536, 100], P('center'), may hold values from -12 to 12
- cotangent: bfloat16 [1024, 100], P('dp'), may hold values from -18 to 18
Outputs:
- predictions: float32 [1024, 100], P(('dp', 'center'))
- grad_first: float32 [2048, 2048], P('dp', 'center')
- grad_bias: float32 [2048], P('center')
- grad_second: float32 [2048, 512], P('center', 'dp')
- grad_centers: float32 [65536, 512], P('center', 'dp')
- grad_coefs: float32 [65536, 100], P('center')
All inputs are finite; a program needn't handle non-finite values.
Results may differ from a plain program's by a relative error of at most 0.028.
Values may be sent and summed in bfloat16 or wider, within the bound.
No kernel may reach another device: no remote copies, remote signals or barrier semaphores. Data moves between devices by JAX's collectives and lax.ppermute only.
A program may use at most 64 MiB of HBM per device.

v0:
```python
import jax
import jax.numpy as jnp
from jax import lax
from jax.sharding import PartitionSpec as P


def body(embeddings, first_weight, first_bias, second_weight, centers, coefficients, cotangent):
    feat_width = centers.shape[1]
    factor = 16.0 / feat_width
    gathered = lax.all_gather(embeddings, "center", axis=1, tiled=True)
    preact = jnp.dot(gathered, first_weight, preferred_element_type=jnp.float32) + first_bias
    hidden = jax.nn.gelu(preact).astype(jnp.bfloat16)
    feature_sum = lax.psum(
        jnp.dot(hidden, second_weight, preferred_element_type=jnp.float32), "center"
    )
    squashed = jnp.tanh(feature_sum)
    features = squashed.astype(jnp.bfloat16)
    feat_wide = features.astype(jnp.float32)
    center_wide = centers.astype(jnp.float32)
    feat_norms = jnp.sum(feat_wide * feat_wide, axis=1)
    center_norms = jnp.sum(center_wide * center_wide, axis=1)
    inner_prods = jnp.einsum("tf,cf->tc", features, centers, preferred_element_type=jnp.float32)
    sq_dist = feat_norms[:, None] + center_norms[None, :] - 2.0 * inner_prods
    kernel = jnp.exp(-8.0 * sq_dist / feat_width).astype(jnp.bfloat16)
    pred_part = jnp.dot(kernel, coefficients, preferred_element_type=jnp.float32)
    kernel_grad = jnp.einsum(
        "to,co->tc", cotangent, coefficients, preferred_element_type=jnp.float32
    )
    weighted = kernel_grad * kernel.astype(jnp.float32)
    weighted_low = weighted.astype(jnp.bfloat16)
    feat_grad_part = -factor * (
        jnp.sum(weighted, axis=1)[:, None] * feat_wide
        - jnp.dot(weighted_low, centers, preferred_element_type=jnp.float32)
    )
    center_grad = -factor * (
        jnp.sum(weighted, axis=0)[:, None] * center_wide
        - jnp.einsum("tc,tf->cf", weighted_low, features, preferred_element_type=jnp.float32)
    )
    coef_grad = jnp.einsum("tc,to->co", kernel, cotangent, preferred_element_type=jnp.float32)
    predictions = lax.psum_scatter(
        pred_part.astype(jnp.bfloat16), "center", scatter_dimension=0, tiled=True
    ).astype(jnp.float32)
    feature_grad = lax.psum(feat_grad_part.astype(jnp.bfloat16), "center").astype(jnp.float32)
    phi_grad = (feature_grad * (1.0 - squashed * squashed)).astype(jnp.bfloat16)
    second_grad = jnp.einsum("th,tf->hf", hidden, phi_grad, preferred_element_type=jnp.float32)
    hidden_grad = jnp.einsum(
        "tf,hf->th", phi_grad, second_weight, preferred_element_type=jnp.float32
    )
    unused, pullback = jax.vjp(jax.nn.gelu, preact)
    preact_grad = pullback(hidden_grad)[0]
    bias_grad = jnp.sum(preact_grad, axis=0)
    preact_low = preact_grad.astype(jnp.bfloat16)
    first_grad = jnp.einsum("ti,th->ih", gathered, preact_low, preferred_element_type=jnp.float32)
    first_grad, second_grad, center_grad = (
        lax.psum_scatter(
            first_grad.astype(jnp.bfloat16), "dp", scatter_dimension=0, tiled=True
        ).astype(jnp.float32),
        lax.psum_scatter(
            second_grad.astype(jnp.bfloat16), "dp", scatter_dimension=1, tiled=True
        ).astype(jnp.float32),
        lax.psum_scatter(
            center_grad.astype(jnp.bfloat16), "dp", scatter_dimension=1, tiled=True
        ).astype(jnp.float32),
    )
    bias_grad, coef_grad = (
        lax.psum(bias_grad.astype(jnp.bfloat16), "dp").astype(jnp.float32),
        lax.psum(coef_grad.astype(jnp.bfloat16), "dp").astype(jnp.float32),
    )
    return (predictions, first_grad, bias_grad, second_grad, center_grad, coef_grad)


def solution(mesh):
    placed = (
        P("dp", "center"),
        P(None, "center"),
        P("center"),
        P("center", None),
        P("center", None),
        P("center", None),
        P("dp", None),
    )
    return jax.shard_map(
        body,
        mesh=mesh,
        in_specs=placed,
        out_specs=(
            P(("dp", "center"), None),
            P("dp", "center"),
            P("center"),
            P("center", "dp"),
            P("center", "dp"),
            P("center", None),
        ),
        check_vma=False,
    )
```

profile of v0, /device:TPU:0, one launch (start us, length us, event | category | flops | bytes accessed | tf_op | source)
XLA Modules:
  0.0 502.4 jit_solution(10667676744632239562)
XLA Ops:
  7.2 0.7 all-gather.2.cloned.1.call-update
  8.0 67.4 %all-gather.2.cloned.1.call-done = bf16[1024,2048]{0,1:T(8,128)(2,1)} async-done(((bf16[1024,64]{0,1:T(8,128)(2,1)}), bf16[1024,2048]{0,1:T(8,128)(2,1)}) %all-gather.2.cloned.1.call-update) | async-done | bytes 4194320 | tf_op jit(solution)/shard_map/all_gather | solution.py:10
  75.3 3.1 convolution_add_fusion
  78.4 1.8 fusion.25
  80.3 0.5 fusion
  80.8 133.9 %all-reduce.3.cloned.1.call-done = f32[1024,512]{1,0:T(8,128)} async-done(((f32[1024,512]{1,0:T(8,128)}), f32[1024,512]{1,0:T(8,128)}) %all-reduce.3.cloned.1.call-update) | async-done | bytes 2097168 | tf_op jit(solution)/shard_map/psum | solution.py:13
  214.7 2.0 fusion.8
  216.7 2.9 exponential_convert_fusion
  219.6 2.0 copy-done.3
  221.6 2.0 convolution_convert_fusion.2
  223.6 0.2 all-reduce.5.cloned.1.call-start
  223.8 3.9 fusion.26
  227.7 1.9 copy-done.10
  229.7 3.3 fusion.11
  233.0 7.2 %fusion.4 = f32[2048,512]{1,0:T(8,128)} fusion(bf16[1024,512]{1,0:T(8,128)(2,1)} %copy-done.6, bf16[2048,512]{1,0:T(8,128)(2,1)S(1)} %copy-done.5, f32[2048]{0:T(1024)S(1)} %get-tuple-element.6, bf16[1024,2048]{1,0:T(8,128)(2,1)} %copy-done.10), kind=kOutput, calls=%fused_computation.8 | convolution fusion | flops 2153775104 | bytes 11542528 | tf_op jit(solution)/shard_map/tc,tf->cf/dot_general | solution.py:37
  240.2 1.6 fusion.5
  241.8 116.3 %reduce-scatter.2.cloned.1.call-done = bf16[32,100]{1,0:T(8,128)(2,1)} async-done(((bf16[1024,100]{1,0:T(8,128)(2,1)}), bf16[32,100]{1,0:T(8,128)(2,1)}) %reduce-scatter.2.cloned.1.call-update) | async-done | bytes 6416 | tf_op jit(solution)/shard_map/reduce_scatter | solution.py:40
  358.1 1.3 convert_element_type.79
  359.4 130.3 %all-reduce.5.cloned.1.call-done = bf16[1024,512]{1,0:T(8,128)(2,1)} async-done(((bf16[1024,512]{1,0:T(8,128)(2,1)}), bf16[1024,512]{1,0:T(8,128)(2,1)}) %all-reduce.5.cloned.1.call-update) | async-done | bytes 1048592 | tf_op jit(solution)/shard_map/psum | solution.py:43
  489.7 1.8 multiply_convert_fusion
  491.6 1.0 fusion.17
  492.5 0.6 fusion.27
  493.1 0.5 convert_element_type.160
  493.6 2.2 fusion.7
  (26 shorter events, 0.2 us)
Async XLA Ops:
  7.2 214.4 %copy-start = (bf16[2048,100]{0,1:T(8,128)(2,1)S(1)}, bf16[2048,100]{0,1:T(8,128)(2,1)}, u32[]{:S(2)}) copy-start(bf16[2048,100]{0,1:T(8,128)(2,1)} %param.12) | copy-start | bytes 1228804
  7.2 71.2 %copy-start.9 = (bf16[64,512]{1,0:T(8,128)(2,1)S(1)}, bf16[64,512]{1,0:T(8,128)(2,1)}, u32[]{:S(2)}) copy-start(bf16[64,512]{1,0:T(8,128)(2,1)} %param.10) | copy-start | bytes 196612
  7.2 68.1 %all-gather.2.cloned.1.call-start = ((), (), s32[]{:S(2)}) async-start(), calls=%async_computation.1 | async-start | bytes 4325376 | tf_op jit(solution)/shard_map/all_gather | solution.py:10
  7.9 72.4 %copy-start.5 = (bf16[2048,512]{1,0:T(8,128)(2,1)S(1)}, bf16[2048,512]{1,0:T(8,128)(2,1)}, u32[]{:S(2)}) copy-start(bf16[2048,512]{1,0:T(8,128)(2,1)} %param.11) | copy-start | bytes 6291460
  7.9 206.8 %all-reduce.3.cloned.1.call-start = ((), (), s32[]{:S(2)}) async-start(), calls=%async_computation.2 | async-start | bytes 4194304 | tf_op jit(solution)/shard_map/psum | solution.py:13
  80.2 277.9 %reduce-scatter.2.cloned.1.call-start = ((), (), s32[]{:S(2)}) async-start(), calls=%async_computation.3 | async-start | bytes 270336 | tf_op jit(solution)/shard_map/reduce_scatter | solution.py:40
  216.7 2.9 copy-start.6
  219.6 2.0 copy-start.3
  221.6 2.2 copy-start.8
  223.6 266.1 %all-reduce.5.cloned.1.call-start = ((), (), s32[]{:S(2)}) async-start(), calls=%async_computation.4 | async-start | bytes 2097152 | tf_op jit(solution)/shard_map/psum | solution.py:43
  223.8 5.9 %copy-start.7 = (bf16[1024,512]{1,0:T(8,128)(2,1)S(1)}, bf16[1024,512]{1,0:T(8,128)(2,1)}, u32[]{:S(2)}) copy-start(bf16[1024,512]{1,0:T(8,128)(2,1)} %copy-done.6) | copy-start | bytes 3145732
  227.7 2.0 copy-start.10
  233.0 7.2 %copy-start.4 = (bf16[1024,2048]{1,0:T(8,128)(2,1)S(1)}, bf16[1024,2048]{1,0:T(8,128)(2,1)}, u32[]{:S(2)}) copy-start(bf16[1024,2048]{1,0:T(8,128)(2,1)} %copy-done.3) | copy-start | bytes 12582916
  240.2 249.5 %copy-start.2 = (f32[1024,512]{1,0:T(8,128)S(1)}, f32[1024,512]{1,0:T(8,128)}, u32[]{:S(2)}) copy-start(f32[1024,512]{1,0:T(8,128)} %all-reduce.3.cloned.1.call-done) | copy-start | bytes 6291460
  489.7 3.9 copy-start.1
Sparse Core Ops, SparseCore 0:
  10.9 64.4 all-gather.1
  81.2 133.4 all-reduce.2
  223.7 134.3 reduce-scatter.1
  363.2 126.5 all-reduce.4
where the time goes:
time: 503 us; the launch traced here: 502 us
  waiting for transfers between devices  449 us (89%)
  matrix products  29.4 us (6%)
  between operations  13.9 us (3%)
  other arithmetic  6.12 us (1%)
    psum x1, waiting for transfers between devices, body(): lax.psum(jnp.dot(hidden, second_weight, preferred_element_type=jnp.float3...  134 us
    psum x1, waiting for transfers between devices, body(): lax.psum(feat_grad_part.astype(jnp.bfloat16), 'center').astype(jnp.float32)  130 us
    reduce_scatter x1, waiting for transfers between devices, body(): lax.psum_scatter(pred_part.astype(jnp.bfloat16), 'center', scatter_dimens...  116 us
    all_gather x1, waiting for transfers between devices, body(): gathered = lax.all_gather(embeddings, 'center', axis=1, tiled=True)  67.4 us
  transfers between devices with their start and end apart: 4, of which 4 were waited for; matrix products, arithmetic and copies ran while one was open for 4% of the time, Pallas kernels for 0%

commit v1 on v0

--- a/solution.py
+++ b/solution.py
@@ -2,6 +2,12 @@
 import jax.numpy as jnp
 from jax import lax
 from jax.sharding import PartitionSpec as P
+
+
+def summed_here(array, name):
+    parts = lax.all_gather(array, name, axis=0, tiled=False)
+    total = parts.sum(axis=0)
+    return total
 
 
 def body(embeddings, first_weight, first_bias, second_weight, centers, coefficients, cotangent):
@@ -40,7 +46,7 @@
     predictions = lax.psum_scatter(
         pred_part.astype(jnp.bfloat16), "center", scatter_dimension=0, tiled=True
     ).astype(jnp.float32)
-    feature_grad = lax.psum(feat_grad_part.astype(jnp.bfloat16), "center").astype(jnp.float32)
+    feature_grad = summed_here(feat_grad_part.astype(jnp.bfloat16), "center").astype(jnp.float32)
     phi_grad = (feature_grad * (1.0 - squashed * squashed)).astype(jnp.bfloat16)
     second_grad = jnp.einsum("th,tf->hf", hidden, phi_grad, preferred_element_type=jnp.float32)
     hidden_grad = jnp.einsum(

time: 503 us -> 576 us (1.15)
  waiting for transfers between devices: 449 us -> 510 us
  other arithmetic: 6.12 us -> 18.6 us
    all_gather x0 -> x1, waiting for transfers between devices: none -> 191 us  [summed_here(): parts = lax.all_gather(array, name, axis=0, tiled=False)]
    psum x1 -> x0, waiting for transfers between devices: 130 us -> none  [body(): lax.psum(feat_grad_part.astype(jnp.bfloat16), 'center').astype(jnp.float32)]
    reduce_sum x0 -> x1, other arithmetic: none -> 12.5 us  [summed_here(): total = parts.sum(axis=0)]
  transfers between devices with their start and end apart: 4 -> 4, of which waited for: 4 -> 4; matrix products, arithmetic and copies ran while one was open for 4% -> 3% of each run, Pallas kernels for 0% -> 0%
where the time goes in v1:
time: 576 us
  waiting for transfers between devices  510 us (89%)
  matrix products  29.1 us (5%)
  other arithmetic  18.6 us (3%)
  between operations  13.9 us (2%)
    all_gather x1, waiting for transfers between devices, summed_here(): parts = lax.all_gather(array, name, axis=0, tiled=False)  191 us
    psum x1, waiting for transfers between devices, body(): lax.psum(jnp.dot(hidden, second_weight, preferred_element_type=jnp.float3...  134 us
    reduce_scatter x1, waiting for transfers between devices, body(): lax.psum_scatter(pred_part.astype(jnp.bfloat16), 'center', scatter_dimens...  117 us
    all_gather x1, waiting for transfers between devices, body(): gathered = lax.all_gather(embeddings, 'center', axis=1, tiled=True)  67.4 us
    reduce_sum x1, other arithmetic, summed_here(): total = parts.sum(axis=0)  12.5 us
  transfers between devices with their start and end apart: 4, of which 4 were waited for; matrix products, arithmetic and copies ran while one was open for 3% of the time, Pallas kernels for 0%

profile of v1, /device:TPU:0, one launch (start us, length us, event | category | flops | bytes accessed | tf_op | source)
XLA Modules:
  0.0 576.1 jit_solution(14120177396860181747)
XLA Ops:
  7.2 0.7 all-gather.4.cloned.1.call-update
  8.0 67.4 %all-gather.4.cloned.1.call-done = bf16[1024,2048]{0,1:T(8,128)(2,1)} async-done(((bf16[1024,64]{0,1:T(8,128)(2,1)}), bf16[1024,2048]{0,1:T(8,128)(2,1)}) %all-gather.4.cloned.1.call-update) | async-done | bytes 4194320 | tf_op jit(solution)/shard_map/all_gather | solution.py:16
  75.3 3.1 convolution_add_fusion
  78.4 1.8 fusion.25
  80.3 0.5 fusion
  80.8 133.9 %all-reduce.2.cloned.1.call-done = f32[1024,512]{1,0:T(8,128)} async-done(((f32[1024,512]{1,0:T(8,128)}), f32[1024,512]{1,0:T(8,128)}) %all-reduce.2.cloned.1.call-update) | async-done | bytes 2097168 | tf_op jit(solution)/shard_map/psum | solution.py:19
  214.7 2.0 fusion.8
  216.7 2.9 exponential_convert_fusion
  219.6 2.0 copy-done.3
  221.7 2.0 convolution_convert_fusion.2
  223.9 3.9 fusion.26
  227.8 2.0 copy-done.10
  229.7 3.3 fusion.11
  233.1 3.9 fusion.5
  237.0 4.6 fusion.4
  241.6 116.6 %reduce-scatter.2.cloned.1.call-done = bf16[32,100]{1,0:T(8,128)(2,1)} async-done(((bf16[1024,100]{1,0:T(8,128)(2,1)}), bf16[32,100]{1,0:T(8,128)(2,1)}) %reduce-scatter.2.cloned.1.call-update) | async-done | bytes 6416 | tf_op jit(solution)/shard_map/reduce_scatter | solution.py:46
  358.2 1.3 convert_element_type.81
  359.5 191.5 %all-gather.6.cloned.1.call-done = bf16[32768,512]{1,0:T(8,128)(2,1)} async-done(((bf16[1024,512]{1,0:T(8,128)(2,1)}), bf16[32768,512]{1,0:T(8,128)(2,1)}) %all-gather.6.cloned.1.call-update) | async-done | bytes 33554448 | tf_op jit(solution)/shard_map/all_gather | solution.py:8
  550.9 12.5 %reduce_sum.60 = bf16[1024,512]{1,0:T(8,128)(2,1)} reduce(bf16[32,1024,512]{2,1,0:T(8,128)(2,1)} %bitcast.23, bf16[]{:T(256)} %constant.24.clone.1), dimensions={0}, to_apply=%region_5.0 | reduce | flops 16252928 | bytes 34603008 | tf_op jit(solution)/shard_map/reduce_sum | solution.py:9
  563.4 1.8 multiply_convert_fusion
  565.3 1.0 fusion.17
  566.2 0.6 fusion.27
  566.8 0.5 convert_element_type.162
  567.3 2.2 fusion.7
  (29 shorter events, 0.4 us)
Async XLA Ops:
  7.2 214.5 %copy-start = (bf16[2048,100]{0,1:T(8,128)(2,1)S(1)}, bf16[2048,100]{0,1:T(8,128)(2,1)}, u32[]{:S(2)}) copy-start(bf16[2048,100]{0,1:T(8,128)(2,1)} %param.12) | copy-start | bytes 1228804
  7.2 71.2 %copy-start.9 = (bf16[64,512]{1,0:T(8,128)(2,1)S(1)}, bf16[64,512]{1,0:T(8,128)(2,1)}, u32[]{:S(2)}) copy-start(bf16[64,512]{1,0:T(8,128)(2,1)} %param.10) | copy-start | bytes 196612
  7.2 68.1 %all-gather.4.cloned.1.call-start = ((), (), s32[]{:S(2)}) async-start(), calls=%async_computation.1 | async-start | bytes 4325376 | tf_op jit(solution)/shard_map/all_gather | solution.py:16
  7.9 72.4 %copy-start.4 = (bf16[2048,512]{1,0:T(8,128)(2,1)S(1)}, bf16[2048,512]{1,0:T(8,128)(2,1)}, u32[]{:S(2)}) copy-start(bf16[2048,512]{1,0:T(8,128)(2,1)} %param.11) | copy-start | bytes 6291460
  7.9 206.8 %all-reduce.2.cloned.1.call-start = ((), (), s32[]{:S(2)}) async-start(), calls=%async_computation.2 | async-start | bytes 4194304 | tf_op jit(solution)/shard_map/psum | solution.py:19
  80.2 277.9 %reduce-scatter.2.cloned.1.call-start = ((), (), s32[]{:S(2)}) async-start(), calls=%async_computation.3 | async-start | bytes 270336 | tf_op jit(solution)/shard_map/reduce_scatter | solution.py:46
  216.7 2.9 copy-start.5
  219.6 2.0 copy-start.3
  221.7 2.2 copy-start.8
  223.6 327.3 %all-gather.6.cloned.1.call-start = ((), (), s32[]{:S(2)}) async-start(), calls=%async_computation.4 | async-start | bytes 34603008 | tf_op jit(solution)/shard_map/all_gather | solution.py:8
  223.9 5.9 %copy-start.6 = (bf16[1024,512]{1,0:T(8,128)(2,1)S(1)}, bf16[1024,512]{1,0:T(8,128)(2,1)}, u32[]{:S(2)}) copy-start(bf16[1024,512]{1,0:T(8,128)(2,1)} %copy-done.5) | copy-start | bytes 3145732
  227.8 2.0 copy-start.10
  233.1 4.0 copy-start.7
  233.1 4.0 copy-start.11
  550.9 12.5 %copy-start.2 = (f32[1024,512]{1,0:T(8,128)S(1)}, f32[1024,512]{1,0:T(8,128)}, u32[]{:S(2)}) copy-start(f32[1024,512]{1,0:T(8,128)} %all-reduce.2.cloned.1.call-done) | copy-start | bytes 6291460
  563.4 3.9 copy-start.1
Sparse Core Ops, SparseCore 0:
  10.9 64.4 all-gather.3
  81.2 133.4 all-reduce.1
  223.8 134.3 reduce-scatter.1
  360.9 190.0 all-gather.5

commit v2 on v0

--- a/solution.py
+++ b/solution.py
@@ -7,7 +7,8 @@
 def body(embeddings, first_weight, first_bias, second_weight, centers, coefficients, cotangent):
     feat_width = centers.shape[1]
     factor = 16.0 / feat_width
-    gathered = lax.all_gather(embeddings, "center", axis=1, tiled=True)
+    parts = lax.all_gather(embeddings, "center", axis=0, tiled=False)
+    gathered = jnp.concatenate(parts, axis=1)
     preact = jnp.dot(gathered, first_weight, preferred_element_type=jnp.float32) + first_bias
     hidden = jax.nn.gelu(preact).astype(jnp.bfloat16)
     feature_sum = lax.psum(

time: 503 us -> 508 us (level)
  local copies, waits for them, and re-layouts: 3.96 us -> 12.9 us
    unnamed x22 -> x29, local copies, waits for them, and re-layouts: 3.96 us -> 10.5 us
where the time goes in v2:
time: 508 us
  waiting for transfers between devices  447 us (88%)
  matrix products  27.2 us (5%)
  between operations  13.9 us (3%)
  local copies, waits for them, and re-layouts  12.9 us (3%)
  other arithmetic  6.11 us (1%)
    psum x1, waiting for transfers between devices, body(): lax.psum(jnp.dot(hidden, second_weight, preferred_element_type=jnp.float3...  133 us
    psum x1, waiting for transfers between devices, body(): lax.psum(feat_grad_part.astype(jnp.bfloat16), 'center').astype(jnp.float32)  130 us
    reduce_scatter x1, waiting for transfers between devices, body(): lax.psum_scatter(pred_part.astype(jnp.bfloat16), 'center', scatter_dimens...  116 us
    all_gather x1, waiting for transfers between devices, body(): parts = lax.all_gather(embeddings, 'center', axis=0, tiled=False)  67.4 us
    unnamed x29, local copies, waits for them, and re-layouts  10.5 us
  transfers between devices with their start and end apart: 4, of which 4 were waited for; matrix products, arithmetic and copies ran while one was open for 4% of the time, Pallas kernels for 0%

profile of v2, /device:TPU:0, one launch (start us, length us, event | category | flops | bytes accessed | tf_op | source)
XLA Modules:
  0.0 507.8 jit_solution(16674384829793613967)
XLA Ops:
  7.2 0.7 all-gather.3.cloned.1.call-update
  8.0 67.4 %all-gather.3.cloned.1.call-done = bf16[32768,64]{0,1:T(8,128)(2,1)} async-done(((bf16[1024,64]{0,1:T(8,128)(2,1)}), bf16[32768,64]{0,1:T(8,128)(2,1)}) %all-gather.3.cloned.1.call-update) | async-done | bytes 4194320 | tf_op jit(solution)/shard_map/all_gather | solution.py:10
  75.4 4.6 copy.14
  80.0 2.3 copy.13
  82.4 1.9 copy-done.1
  84.3 0.8 convolution_add_fusion
  85.2 1.8 fusion.25
  87.5 133.0 %all-reduce.3.cloned.1.call-done = f32[1024,512]{1,0:T(8,128)} async-done(((f32[1024,512]{1,0:T(8,128)}), f32[1024,512]{1,0:T(8,128)}) %all-reduce.3.cloned.1.call-update) | async-done | bytes 2097168 | tf_op jit(solution)/shard_map/psum | solution.py:14
  220.5 2.0 fusion.8
  222.5 2.9 exponential_convert_fusion
  225.5 2.0 copy-done.4
  227.4 2.0 convolution_convert_fusion.2
  229.7 3.9 fusion.26
  233.5 2.0 copy-done.13
  235.5 3.3 fusion.11
  238.9 7.2 %fusion.4 = f32[2048,512]{1,0:T(8,128)} fusion(bf16[1024,512]{1,0:T(8,128)(2,1)} %copy-done.7, bf16[2048,512]{1,0:T(8,128)(2,1)S(1)} %copy-done.6, f32[2048]{0:T(1024)S(1)} %get-tuple-element.6, bf16[1024,2048]{1,0:T(8,128)(2,1)} %copy-done.13), kind=kOutput, calls=%fused_computation.8 | convolution fusion | flops 2153775104 | bytes 11542528 | tf_op jit(solution)/shard_map/tc,tf->cf/dot_general | solution.py:38
  246.0 1.6 fusion.5
  247.7 115.8 %reduce-scatter.2.cloned.1.call-done = bf16[32,100]{1,0:T(8,128)(2,1)} async-done(((bf16[1024,100]{1,0:T(8,128)(2,1)}), bf16[32,100]{1,0:T(8,128)(2,1)}) %reduce-scatter.2.cloned.1.call-update) | async-done | bytes 6416 | tf_op jit(solution)/shard_map/reduce_scatter | solution.py:41
  363.5 1.3 convert_element_type.79
  364.8 130.3 %all-reduce.5.cloned.1.call-done = bf16[1024,512]{1,0:T(8,128)(2,1)} async-done(((bf16[1024,512]{1,0:T(8,128)(2,1)}), bf16[1024,512]{1,0:T(8,128)(2,1)}) %all-reduce.5.cloned.1.call-update) | async-done | bytes 1048592 | tf_op jit(solution)/shard_map/psum | solution.py:44
  495.2 1.8 multiply_convert_fusion
  497.0 1.0 fusion.17
  498.0 0.6 fusion.27
  498.6 2.2 fusion.7
  (34 shorter events, 1.4 us)
Async XLA Ops:
  7.2 220.3 %copy-start = (bf16[2048,100]{0,1:T(8,128)(2,1)S(1)}, bf16[2048,100]{0,1:T(8,128)(2,1)}, u32[]{:S(2)}) copy-start(bf16[2048,100]{0,1:T(8,128)(2,1)} %param.12) | copy-start | bytes 1228804
  7.2 68.2 %all-gather.3.cloned.1.call-start = ((), (), s32[]{:S(2)}) async-start(), calls=%async_computation.4 | async-start | bytes 4325376 | tf_op jit(solution)/shard_map/all_gather | solution.py:10
  7.9 212.6 %all-reduce.3.cloned.1.call-start = ((), (), s32[]{:S(2)}) async-start(), calls=%async_computation.1 | async-start | bytes 4194304 | tf_op jit(solution)/shard_map/psum | solution.py:14
  80.0 4.3 copy-start.9
  80.0 4.3 copy-start.12
  82.4 1.9 copy-start.1
  82.4 2.8 copy-start.11
  84.3 2.7 copy-start.6
  87.0 276.5 %reduce-scatter.2.cloned.1.call-start = ((), (), s32[]{:S(2)}) async-start(), calls=%async_computation.2 | async-start | bytes 270336 | tf_op jit(solution)/shard_map/reduce_scatter | solution.py:41
  222.5 2.9 copy-start.7
  225.5 2.0 copy-start.4
  227.4 2.2 copy-start.10
  229.4 265.8 %all-reduce.5.cloned.1.call-start = ((), (), s32[]{:S(2)}) async-start(), calls=%async_computation.3 | async-start | bytes 2097152 | tf_op jit(solution)/shard_map/psum | solution.py:44
  229.7 5.8 %copy-start.8 = (bf16[1024,512]{1,0:T(8,128)(2,1)S(1)}, bf16[1024,512]{1,0:T(8,128)(2,1)}, u32[]{:S(2)}) copy-start(bf16[1024,512]{1,0:T(8,128)(2,1)} %copy-done.7) | copy-start | bytes 3145732
  233.5 2.0 copy-start.13
  238.8 7.2 %copy-start.5 = (bf16[1024,2048]{1,0:T(8,128)(2,1)S(1)}, bf16[1024,2048]{1,0:T(8,128)(2,1)}, u32[]{:S(2)}) copy-start(bf16[1024,2048]{1,0:T(8,128)(2,1)} %copy-done.4) | copy-start | bytes 12582916
  246.0 249.1 %copy-start.3 = (f32[1024,512]{1,0:T(8,128)S(1)}, f32[1024,512]{1,0:T(8,128)}, u32[]{:S(2)}) copy-start(f32[1024,512]{1,0:T(8,128)} %all-reduce.3.cloned.1.call-done) | copy-start | bytes 6291460
  495.2 3.4 copy-start.2
Sparse Core Ops, SparseCore 0:
  10.9 64.4 all-gather.2
  87.1 133.3 all-reduce.2
  229.5 133.9 reduce-scatter.1
  368.6 126.5 all-reduce.4
